TPU v7x, 32 devices: a whole 2x2x4 slice. The times are simulated.
32 devices in a mesh: tok: 4 (over x, core), vocab: 8 (over z, y).
Axes of the slice: x: 2, y: 2, z: 4, core: 2. Of those that a mesh axis runs over, the one named last changes fastest.
Arguments:
- hidden_states: bfloat16 [512, 3584], P('tok'), may hold values from -6 to 6, as said below
- hidden_tangent: bfloat16 [512, 3584], P('tok'), may hold values from -6 to 6
- buckets: int32 [512], P('tok'), may hold values from 0 to 7
- head_weight: bfloat16 [3584, 5120], P(None, 'vocab')
Outputs:
- hidden_cotangent: bfloat16 [3584, 512], P('vocab', 'tok')
- weight_gradient: bfloat16 [3584, 5120], P('tok', 'vocab')
Inputs may be any that keep to these rules, and one draw needn't show every extreme that they name: `hidden_states`: hidden states of order one.
All inputs are finite; a program needn't handle non-finite values.
Results may differ from a plain program's by a relative error of at most 0.0107.
Values may be sent and summed in bfloat16 or wider, within the bound.
A program may use at most 64 MiB of HBM per device.

v0:
```python
import jax
import jax.numpy as jnp
from jax import lax
from jax.sharding import PartitionSpec as P

TOK_DEV = 128
BUCKETS = 8


def local(hidden_states, hidden_tangent, buckets, head_weight):
    logits = jnp.dot(hidden_states, head_weight, preferred_element_type=jnp.float32)
    tangent = jnp.dot(hidden_tangent, head_weight, preferred_element_type=jnp.float32)
    peak = lax.pmax(jnp.max(logits, axis=1), "vocab")
    expo = jnp.exp(logits - peak[:, None])
    total = lax.psum(jnp.sum(expo, axis=1), "vocab")
    probs = expo / total[:, None]
    mean = lax.psum(jnp.sum(probs * tangent, axis=1), "vocab")
    scale = 0.25 * jnp.exp2(buckets.astype(jnp.float32) * (3.0 / (BUCKETS - 1)))
    grads = (scale[:, None] * probs * (tangent - mean[:, None])).astype(jnp.bfloat16)
    width = head_weight.shape[0]
    cotan = lax.psum_scatter(
        lax.dot_general(
            head_weight, grads, (((1,), (1,)), ((), ())), preferred_element_type=jnp.float32
        ),
        "vocab",
        scatter_dimension=0,
        tiled=True,
    )
    hidden_cotangent = cotan.astype(jnp.bfloat16)
    feature_rows = width // lax.axis_size("tok")
    column_start = lax.axis_index("tok") * feature_rows
    pieces = (
        lax.all_gather(hidden_states, "tok", axis=0, tiled=True),
        lax.all_gather(grads, "tok", axis=0, tiled=True),
    )
    columns = lax.dynamic_slice_in_dim(pieces[0], column_start, feature_rows, 1)
    blocks_h = columns.reshape(-1, TOK_DEV, feature_rows)
    blocks_g = pieces[1].reshape(-1, TOK_DEV, pieces[1].shape[1])
    partial_terms = jnp.einsum(
        "kti,ktv->kiv", blocks_h, blocks_g, preferred_element_type=jnp.float32
    ).astype(jnp.bfloat16)
    summed = jnp.sum(partial_terms.astype(jnp.float32), axis=0)
    return (hidden_cotangent, summed.astype(jnp.bfloat16))


def solution(mesh):
    return jax.shard_map(
        local,
        mesh=mesh,
        in_specs=(P("tok", None), P("tok", None), P("tok"), P(None, "vocab")),
        out_specs=(P("vocab", "tok"), P("tok", "vocab")),
        check_vma=False,
    )
```

profile of v0, /device:TPU:0, one launch (start us, length us, event | category | flops | bytes accessed | tf_op | source)
XLA Modules:
  0.0 158.0 jit_solution(476871489584601557)
XLA Ops:
  8.0 0.0 copy-start
  8.0 0.0 reduce-scatter.4.cloned.1.call-start
  8.1 0.7 exponential_multiply_fusion
  8.8 3.6 %fusion.2 = (f32[128]{0:T(128)S(1)}, f32[128,640]{1,0:T(8,128)S(1)}) fusion(bf16[128,3584]{1,0:T(8,128)(2,1)} %param.4, bf16[3584,640]{1,0:T(8,128)(2,1)} %param.7), kind=kOutput, calls=%fused_computation.9 | convolution fusion | flops 587284352 | bytes 5833216 | tf_op jit(solution)/shard_map/dot_general | solution.py:11
  12.3 23.2 %pmax.7 = f32[128]{0:T(128)S(1)} all-reduce(f32[128]{0:T(128)S(1)} %get-tuple-element.8), channel_id=1, replica_groups=mesh['tok'=4,'vocab'=8] {'vocab'}, use_global_device_ids=true, to_apply=%region_1.0 | all-reduce | flops 128 | bytes 1024 | tf_op jit(solution)/shard_map/pmax | solution.py:13
  35.5 0.2 fusion.1
  35.7 17.1 %psum.14 = f32[128]{0:T(128)S(1)} all-reduce(f32[128]{0:T(128)S(1)} %fusion.1), channel_id=1, replica_groups=mesh['tok'=4,'vocab'=8] {'vocab'}, use_global_device_ids=true, to_apply=%region_3.0 | all-reduce | flops 128 | bytes 1024 | tf_op jit(solution)/shard_map/psum | solution.py:15
  52.8 0.0 copy-done
  52.8 3.3 %multiply_reduce_fusion = (f32[128]{0:T(128)S(1)}, f32[128,640]{1,0:T(8,128)S(1)}) fusion(f32[128]{0:T(128)S(1)} %psum.14, f32[128,640]{1,0:T(8,128)S(1)} %get-tuple-element.9, f32[128]{0:T(128)S(1)} %pmax.7, bf16[128,3584]{1,0:T(8,128)(2,1)S(1)} %copy-done, bf16[3584,640]{1,0:T(8,128)(2,1)} %param.7), kind=kOutput, calls=%fused_computation.3 | convolution fusion | flops 587530112 | bytes 6161920 | tf_op jit(solution)/shard_map/dot_general | solution.py:12
  56.1 19.1 %psum.15 = f32[128]{0:T(128)S(1)} all-reduce(f32[128]{0:T(128)S(1)} %get-tuple-element.10), channel_id=1, replica_groups=mesh['tok'=4,'vocab'=8] {'vocab'}, use_global_device_ids=true, to_apply=%region_5.0 | all-reduce | flops 128 | bytes 1024 | tf_op jit(solution)/shard_map/psum | solution.py:17
  75.2 0.2 multiply_convert_fusion
  75.4 3.9 %convolution_bitcast_fusion = f32[3584,128]{0,1:T(8,128)S(1)} fusion(bf16[128,640]{1,0:T(8,128)(2,1)S(1)} %multiply_convert_fusion, bf16[3584,640]{1,0:T(8,128)(2,1)} %param.7), kind=kOutput, calls=%fused_computation | convolution fusion | flops 587202560 | bytes 6586368 | tf_op jit(solution)/shard_map/dot_general | solution.py:22
  79.3 1.7 %copy.12 = f32[3584,128]{1,0:T(8,128)} copy(f32[3584,128]{0,1:T(8,128)S(1)} %convolution_bitcast_fusion) | data formatting | bytes 3670016
  81.0 0.0 reduce-scatter.4.cloned.1.call-update
  81.0 0.0 all-gather.2.cloned.1.call-start
  81.0 0.5 all-gather.2.cloned.1.call-update
  81.6 7.9 %all_gather.7 = bf16[512,640]{1,0:T(8,128)(2,1)S(1)} all-gather(bf16[128,640]{1,0:T(8,128)(2,1)S(1)} %multiply_convert_fusion), channel_id=1, replica_groups=mesh['tok'=4,'vocab'=8] {'tok'}, dimensions={0}, use_global_device_ids=true | all-gather | bytes 819200 | tf_op jit(solution)/shard_map/all_gather | solution.py:34
  89.5 55.5 %reduce-scatter.4.cloned.1.call-done = f32[448,128]{1,0:T(8,128)} async-done(((f32[3584,128]{1,0:T(8,128)}), f32[448,128]{1,0:T(8,128)}) %reduce-scatter.4.cloned.1.call-update) | async-done | bytes 229392
  145.0 1.0 copy.13
  146.1 0.8 copy.10
  146.8 0.0 all-gather.2.cloned.1.call-done
  146.8 1.3 constant_dynamic-slice_fusion
  148.1 2.4 %convert_reduce_fusion = bf16[896,640]{1,0:T(8,128)(2,1)} fusion(bf16[4,128,896]{2,1,0:T(8,128)(2,1)S(1)} %bitcast.13, bf16[4,128,640]{2,1,0:T(8,128)(2,1)S(1)} %bitcast.14), kind=kOutput, calls=%fused_computation.1 | convolution fusion | flops 591216640 | bytes 2719744 | tf_op jit(solution)/shard_map/kti,ktv->kiv/dot_general | solution.py:39
Async XLA Ops:
  8.0 44.8 %copy-start = (bf16[128,3584]{1,0:T(8,128)(2,1)S(1)}, bf16[128,3584]{1,0:T(8,128)(2,1)}, u32[]{:S(2)}) copy-start(bf16[128,3584]{1,0:T(8,128)(2,1)} %param.5) | copy-start | bytes 2752516
  8.0 137.0 %reduce-scatter.4.cloned.1.call-start = ((), (), s32[]{:S(2)}) async-start(), calls=%async_computation.2 | async-start | bytes 2064384
  81.0 65.9 %all-gather.2.cloned.1.call-start = ((), (), s32[]{:S(2)}) async-start(), calls=%async_computation.1 | async-start | bytes 4587520 | tf_op jit(solution)/shard_map/all_gather | solution.py:33
Sparse Core Ops, SparseCore 0:
  81.1 63.8 reduce-scatter.3
Sparse Core Ops, SparseCore 1:
  83.0 28.6 all-gather.1
where the time goes:
time: 158 us
  blocking collectives  67.4 us (43%)
  waiting for transfers between devices  56.1 us (36%)
  between operations  15.5 us (10%)
  matrix products  13.1 us (8%)
  local copies, waits for them, and re-layouts  4.77 us (3%)
    unnamed x3, waiting for transfers between devices  56.1 us
    pmax x1, blocking collectives, local(): peak = lax.pmax(jnp.max(logits, axis=1), 'vocab')  23.2 us
    psum x1, blocking collectives, local(): mean = lax.psum(jnp.sum(probs * tangent, axis=1), 'vocab')  19.1 us
    psum x1, blocking collectives, local(): total = lax.psum(jnp.sum(expo, axis=1), 'vocab')  17.1 us
    all_gather x1, blocking collectives, local(): lax.all_gather(grads, 'tok', axis=0, tiled=True)  7.94 us
    dot_general x1, matrix products, local(): lax.dot_general(head_weight, grads, (((1,), (1,)), ((), ())), preferred_e...  3.85 us
    dot_general x1, matrix products, local(): jnp.dot(hidden_states, head_weight, preferred_element_type=jnp.float32)  3.55 us
    unnamed x5, local copies, waits for them, and re-layouts  3.52 us
  transfers between devices with their start and end apart: 2, of which 1 were waited for; matrix products, arithmetic and copies ran while one was open for 1% of the time, Pallas kernels for 0%

commit v1 on v0

--- a/solution.py
+++ b/solution.py
@@ -14,7 +14,7 @@
     expo = jnp.exp(logits - peak[:, None])
     total = lax.psum(jnp.sum(expo, axis=1), "vocab")
     probs = expo / total[:, None]
-    mean = lax.psum(jnp.sum(probs * tangent, axis=1), "vocab")
+    mean = jnp.sum(lax.all_gather(jnp.sum(probs * tangent, axis=1), "vocab"), axis=0)
     scale = 0.25 * jnp.exp2(buckets.astype(jnp.float32) * (3.0 / (BUCKETS - 1)))
     grads = (scale[:, None] * probs * (tangent - mean[:, None])).astype(jnp.bfloat16)
     width = head_weight.shape[0]

time: 158 us -> 158 us (level)
    psum x1 -> x0, blocking collectives: 19.1 us -> none  [local(): mean = lax.psum(jnp.sum(probs * tangent, axis=1), 'vocab')]
    all_gather x0 -> x1, blocking collectives: none -> 18.3 us  [local(): lax.all_gather(jnp.sum(probs * tangent, axis=1), 'vocab')]
where the time goes in v1:
time: 158 us; the launch traced here: 157 us
  blocking collectives  66.5 us (42%)
  waiting for transfers between devices  56.1 us (36%)
  between operations  15.5 us (10%)
  matrix products  13.1 us (8%)
  local copies, waits for them, and re-layouts  4.77 us (3%)
    unnamed x3, waiting for transfers between devices  56.1 us
    pmax x1, blocking collectives, local(): peak = lax.pmax(jnp.max(logits, axis=1), 'vocab')  23.2 us
    all_gather x1, blocking collectives, local(): lax.all_gather(jnp.sum(probs * tangent, axis=1), 'vocab')  18.3 us
    psum x1, blocking collectives, local(): total = lax.psum(jnp.sum(expo, axis=1), 'vocab')  17.1 us
    all_gather x1, blocking collectives, local(): lax.all_gather(grads, 'tok', axis=0, tiled=True)  7.94 us
    dot_general x1, matrix products, local(): lax.dot_general(head_weight, grads, (((1,), (1,)), ((), ())), preferred_e...  3.85 us
    dot_general x1, matrix products, local(): jnp.dot(hidden_states, head_weight, preferred_element_type=jnp.float32)  3.55 us
    unnamed x5, local copies, waits for them, and re-layouts  3.52 us
  transfers between devices with their start and end apart: 2, of which 1 were waited for; matrix products, arithmetic and copies ran while one was open for 1% of the time, Pallas kernels for 0%

profile of v1, /device:TPU:0, one launch (start us, length us, event | category | flops | bytes accessed | tf_op | source)
XLA Modules:
  0.0 157.2 jit_solution(11065419158914338392)
XLA Ops:
  8.0 0.0 copy-start
  8.0 0.0 reduce-scatter.4.cloned.1.call-start
  8.1 0.7 exponential_multiply_fusion
  8.8 3.6 %fusion.2 = (f32[128]{0:T(128)S(1)}, f32[128,640]{1,0:T(8,128)S(1)}) fusion(bf16[128,3584]{1,0:T(8,128)(2,1)} %param.4, bf16[3584,640]{1,0:T(8,128)(2,1)} %param.7), kind=kOutput, calls=%fused_computation.9 | convolution fusion | flops 587284352 | bytes 5833216 | tf_op jit(solution)/shard_map/dot_general | solution.py:11
  12.3 23.2 %pmax.7 = f32[128]{0:T(128)S(1)} all-reduce(f32[128]{0:T(128)S(1)} %get-tuple-element.8), channel_id=1, replica_groups=mesh['tok'=4,'vocab'=8] {'vocab'}, use_global_device_ids=true, to_apply=%region_1.0 | all-reduce | flops 128 | bytes 1024 | tf_op jit(solution)/shard_map/pmax | solution.py:13
  35.5 0.2 fusion.1
  35.7 17.1 %psum.7 = f32[128]{0:T(128)S(1)} all-reduce(f32[128]{0:T(128)S(1)} %fusion.1), channel_id=1, replica_groups=mesh['tok'=4,'vocab'=8] {'vocab'}, use_global_device_ids=true, to_apply=%region_3.0 | all-reduce | flops 128 | bytes 1024 | tf_op jit(solution)/shard_map/psum | solution.py:15
  52.8 0.0 copy-done
  52.8 3.3 %multiply_reduce_fusion = (f32[128]{0:T(128)S(1)}, f32[128,640]{1,0:T(8,128)S(1)}) fusion(f32[128]{0:T(128)S(1)} %psum.7, f32[128,640]{1,0:T(8,128)S(1)} %get-tuple-element.9, f32[128]{0:T(128)S(1)} %pmax.7, bf16[128,3584]{1,0:T(8,128)(2,1)S(1)} %copy-done, bf16[3584,640]{1,0:T(8,128)(2,1)} %param.7), kind=kOutput, calls=%fused_computation.3 | convolution fusion | flops 587530112 | bytes 6161920 | tf_op jit(solution)/shard_map/dot_general | solution.py:12
  56.1 18.3 %all-gather.1 = f32[8,1,128]{2,1,0:T(1,128)S(1)} all-gather(f32[1,1,128]{2,1,0:T(1,128)S(1)} %bitcast.16), channel_id=2, replica_groups=mesh['tok'=4,'vocab'=8] {'vocab'}, dimensions={0}, use_global_device_ids=true | all-gather | bytes 4608 | tf_op jit(solution)/shard_map/all_gather | solution.py:17
  74.4 0.2 multiply_convert_fusion
  74.6 3.9 %convolution_bitcast_fusion = f32[3584,128]{0,1:T(8,128)S(1)} fusion(bf16[128,640]{1,0:T(8,128)(2,1)S(1)} %multiply_convert_fusion, bf16[3584,640]{1,0:T(8,128)(2,1)} %param.7), kind=kOutput, calls=%fused_computation | convolution fusion | flops 587202560 | bytes 6586368 | tf_op jit(solution)/shard_map/dot_general | solution.py:22
  78.4 1.7 %copy.12 = f32[3584,128]{1,0:T(8,128)} copy(f32[3584,128]{0,1:T(8,128)S(1)} %convolution_bitcast_fusion) | data formatting | bytes 3670016
  80.1 0.0 reduce-scatter.4.cloned.1.call-update
  80.2 0.0 all-gather.4.cloned.1.call-start
  80.2 0.5 all-gather.4.cloned.1.call-update
  80.7 7.9 %all_gather.15 = bf16[512,640]{1,0:T(8,128)(2,1)S(1)} all-gather(bf16[128,640]{1,0:T(8,128)(2,1)S(1)} %multiply_convert_fusion), channel_id=1, replica_groups=mesh['tok'=4,'vocab'=8] {'tok'}, dimensions={0}, use_global_device_ids=true | all-gather | bytes 819200 | tf_op jit(solution)/shard_map/all_gather | solution.py:34
  88.7 55.6 %reduce-scatter.4.cloned.1.call-done = f32[448,128]{1,0:T(8,128)} async-done(((f32[3584,128]{1,0:T(8,128)}), f32[448,128]{1,0:T(8,128)}) %reduce-scatter.4.cloned.1.call-update) | async-done | bytes 229392
  144.3 1.0 copy.13
  145.3 0.8 copy.10
  146.1 0.0 all-gather.4.cloned.1.call-done
  146.1 1.3 constant_dynamic-slice_fusion
  147.4 2.4 %convert_reduce_fusion = bf16[896,640]{1,0:T(8,128)(2,1)} fusion(bf16[4,128,896]{2,1,0:T(8,128)(2,1)S(1)} %bitcast.14, bf16[4,128,640]{2,1,0:T(8,128)(2,1)S(1)} %bitcast.15), kind=kOutput, calls=%fused_computation.1 | convolution fusion | flops 591216640 | bytes 2719744 | tf_op jit(solution)/shard_map/kti,ktv->kiv/dot_general | solution.py:39
  (1 shorter events, 0.0 us)
Async XLA Ops:
  8.0 44.8 %copy-start = (bf16[128,3584]{1,0:T(8,128)(2,1)S(1)}, bf16[128,3584]{1,0:T(8,128)(2,1)}, u32[]{:S(2)}) copy-start(bf16[128,3584]{1,0:T(8,128)(2,1)} %param.5) | copy-start | bytes 2752516
  8.0 136.3 %reduce-scatter.4.cloned.1.call-start = ((), (), s32[]{:S(2)}) async-start(), calls=%async_computation.2 | async-start | bytes 2064384
  80.2 65.9 %all-gather.4.cloned.1.call-start = ((), (), s32[]{:S(2)}) async-start(), calls=%async_computation.1 | async-start | bytes 4587520 | tf_op jit(solution)/shard_map/all_gather | solution.py:33
Sparse Core Ops, SparseCore 0:
  80.3 63.9 reduce-scatter.3
Sparse Core Ops, SparseCore 1:
  82.2 28.6 all-gather.3

commit v2 on v0

--- a/solution.py
+++ b/solution.py
@@ -5,6 +5,23 @@
 
 TOK_DEV = 128
 BUCKETS = 8
+
+
+def in_order(pieces, dim):
+    pieces = jnp.moveaxis(pieces, 0, dim)
+    shape = pieces.shape
+    return pieces.reshape(*shape[:dim], shape[dim] * shape[dim + 1], *shape[dim + 2 :])
+
+
+def collect(x, axis, dim):
+    size = lax.axis_size(axis)
+    ahead = [(i, (i + 1) % size) for i in range(size)]
+    blocks = [x]
+    while len(blocks) < size:
+        blocks.append(lax.ppermute(blocks[-1], axis, ahead))
+    here = lax.axis_index(axis)
+    blocks = jnp.stack(blocks)[(here - jnp.arange(size)) % size]
+    return in_order(blocks, dim)
 
 
 def local(hidden_states, hidden_tangent, buckets, head_weight):
@@ -29,10 +46,7 @@
     hidden_cotangent = cotan.astype(jnp.bfloat16)
     feature_rows = width // lax.axis_size("tok")
     column_start = lax.axis_index("tok") * feature_rows
-    pieces = (
-        lax.all_gather(hidden_states, "tok", axis=0, tiled=True),
-        lax.all_gather(grads, "tok", axis=0, tiled=True),
-    )
+    pieces = (lax.all_gather(hidden_states, "tok", axis=0, tiled=True), collect(grads, "tok", 0))
     columns = lax.dynamic_slice_in_dim(pieces[0], column_start, feature_rows, 1)
     blocks_h = columns.reshape(-1, TOK_DEV, feature_rows)
     blocks_g = pieces[1].reshape(-1, TOK_DEV, pieces[1].shape[1])

time: 158 us -> 158 us (level)
  blocking collectives: 67.4 us -> 59.4 us
  waiting for transfers between devices: 56.1 us -> 61.7 us
    ppermute x0 -> x3, waiting for transfers between devices: none -> 17.5 us  [collect(): blocks.append(lax.ppermute(blocks[-1], axis, ahead))]
    unnamed x3, waiting for transfers between devices: 56.1 us -> 44.2 us
    all_gather x1 -> x0, blocking collectives: 7.94 us -> none  [local(): lax.all_gather(grads, 'tok', axis=0, tiled=True)]
  transfers between devices with their start and end apart: 2 -> 5, of which waited for: 1 -> 4; matrix products, arithmetic and copies ran while one was open for 1% -> 2% of each run, Pallas kernels for 0% -> 0%
where the time goes in v2:
time: 158 us
  waiting for transfers between devices  61.7 us (39%)
  blocking collectives  59.4 us (38%)
  between operations  15.5 us (10%)
  matrix products  13.1 us (8%)
  local copies, waits for them, and re-layouts  5.43 us (3%)
  starting transfers between devices  1.61 us (1%)
    unnamed x3, waiting for transfers between devices  44.2 us
    pmax x1, blocking collectives, local(): peak = lax.pmax(jnp.max(logits, axis=1), 'vocab')  23.2 us
    psum x1, blocking collectives, local(): mean = lax.psum(jnp.sum(probs * tangent, axis=1), 'vocab')  19.1 us
    ppermute x3, waiting for transfers between devices, collect(): blocks.append(lax.ppermute(blocks[-1], axis, ahead))  17.5 us
    psum x1, blocking collectives, local(): total = lax.psum(jnp.sum(expo, axis=1), 'vocab')  17.1 us
    dot_general x1, matrix products, local(): lax.dot_general(head_weight, grads, (((1,), (1,)), ((), ())), preferred_e...  3.85 us
    dot_general x1, matrix products, local(): jnp.dot(hidden_states, head_weight, preferred_element_type=jnp.float32)  3.55 us
    unnamed x5, local copies, waits for them, and re-layouts  3.52 us
  transfers between devices with their start and end apart: 5, of which 4 were waited for; matrix products, arithmetic and copies ran while one was open for 2% of the time, Pallas kernels for 0%

profile of v2, /device:TPU:0, one launch (start us, length us, event | category | flops | bytes accessed | tf_op | source)
XLA Modules:
  0.0 158.0 jit_solution(12264140219183082992)
XLA Ops:
  8.1 0.7 exponential_multiply_fusion
  8.8 3.6 %fusion.4 = (f32[128]{0:T(128)S(1)}, f32[128,640]{1,0:T(8,128)S(1)}) fusion(bf16[128,3584]{1,0:T(8,128)(2,1)} %param.4, bf16[3584,640]{1,0:T(8,128)(2,1)} %param.7), kind=kOutput, calls=%fused_computation.18 | convolution fusion | flops 587284352 | bytes 5833216 | tf_op jit(solution)/shard_map/dot_general | solution.py:28
  12.3 23.2 %pmax.7 = f32[128]{0:T(128)S(1)} all-reduce(f32[128]{0:T(128)S(1)} %get-tuple-element.8), channel_id=1, replica_groups=mesh['tok'=4,'vocab'=8] {'vocab'}, use_global_device_ids=true, to_apply=%region_1.0 | all-reduce | flops 128 | bytes 1024 | tf_op jit(solution)/shard_map/pmax | solution.py:30
  35.5 0.2 fusion.1
  35.7 17.1 %psum.14 = f32[128]{0:T(128)S(1)} all-reduce(f32[128]{0:T(128)S(1)} %fusion.1), channel_id=1, replica_groups=mesh['tok'=4,'vocab'=8] {'vocab'}, use_global_device_ids=true, to_apply=%region_3.0 | all-reduce | flops 128 | bytes 1024 | tf_op jit(solution)/shard_map/psum | solution.py:32
  52.8 3.3 %multiply_reduce_fusion = (f32[128]{0:T(128)S(1)}, f32[128,640]{1,0:T(8,128)S(1)}) fusion(f32[128]{0:T(128)S(1)} %psum.14, f32[128,640]{1,0:T(8,128)S(1)} %get-tuple-element.9, f32[128]{0:T(128)S(1)} %pmax.7, bf16[128,3584]{1,0:T(8,128)(2,1)S(1)} %copy-done, bf16[3584,640]{1,0:T(8,128)(2,1)} %param.7), kind=kOutput, calls=%fused_computation.5 | convolution fusion | flops 587530112 | bytes 6161920 | tf_op jit(solution)/shard_map/dot_general | solution.py:29
  56.1 19.1 %psum.15 = f32[128]{0:T(128)S(1)} all-reduce(f32[128]{0:T(128)S(1)} %get-tuple-element.10), channel_id=1, replica_groups=mesh['tok'=4,'vocab'=8] {'vocab'}, use_global_device_ids=true, to_apply=%region_5.0 | all-reduce | flops 128 | bytes 1024 | tf_op jit(solution)/shard_map/psum | solution.py:34
  75.2 0.2 multiply_convert_fusion
  75.4 3.9 %convolution_bitcast_fusion = f32[3584,128]{0,1:T(8,128)S(1)} fusion(bf16[128,640]{1,0:T(8,128)(2,1)S(1)} %multiply_convert_fusion, bf16[3584,640]{1,0:T(8,128)(2,1)} %param.7), kind=kOutput, calls=%fused_computation.1 | convolution fusion | flops 587202560 | bytes 6586368 | tf_op jit(solution)/shard_map/dot_general | solution.py:39
  79.3 1.7 %copy.12 = f32[3584,128]{1,0:T(8,128)} copy(f32[3584,128]{0,1:T(8,128)S(1)} %convolution_bitcast_fusion) | data formatting | bytes 3670016
  81.0 0.0 all-gather.2.cloned.1.call-start
  81.0 0.5 all-gather.2.cloned.1.call-update
  81.6 0.1 collective-permute-start
  81.6 4.7 %collective-permute-done = bf16[128,640]{1,0:T(8,128)(2,1)S(1)} collective-permute-done((bf16[128,640]{1,0:T(8,128)(2,1)S(1)}, bf16[128,640]{1,0:T(8,128)(2,1)S(1)}, u32[]{:S(2)}, u32[]{:S(2)}) %collective-permute-start) | collective-permute-done | bytes 163872 | tf_op jit(solution)/shard_map/ppermute | solution.py:21
  86.4 5.9 %collective-permute-done.1 = bf16[128,640]{1,0:T(8,128)(2,1)S(1)} collective-permute-done((bf16[128,640]{1,0:T(8,128)(2,1)S(1)}, bf16[128,640]{1,0:T(8,128)(2,1)S(1)}, u32[]{:S(2)}, u32[]{:S(2)}) %collective-permute-start.1) | collective-permute-done | bytes 163872 | tf_op jit(solution)/shard_map/ppermute | solution.py:21
  92.2 1.5 collective-permute-start.2
  93.7 6.9 %collective-permute-done.2 = bf16[128,640]{1,0:T(8,128)(2,1)S(1)} collective-permute-done((bf16[128,640]{1,0:T(8,128)(2,1)S(1)}, bf16[128,640]{1,0:T(8,128)(2,1)S(1)}, u32[]{:S(2)}, u32[]{:S(2)}) %collective-permute-start.2) | collective-permute-done | bytes 163872 | tf_op jit(solution)/shard_map/ppermute | solution.py:21
  100.6 0.1 pad_maximum_fusion
  100.7 0.7 gather_fusion
  101.4 43.6 %reduce-scatter.4.cloned.1.call-done = f32[448,128]{1,0:T(8,128)} async-done(((f32[3584,128]{1,0:T(8,128)}), f32[448,128]{1,0:T(8,128)}) %reduce-scatter.4.cloned.1.call-update) | async-done | bytes 229392
  145.0 1.0 copy.13
  146.1 0.8 copy.10
  146.8 1.3 constant_dynamic-slice_fusion
  148.1 2.4 %convert_reduce_fusion = bf16[896,640]{1,0:T(8,128)(2,1)} fusion(bf16[4,128,896]{2,1,0:T(8,128)(2,1)S(1)} %bitcast.19, bf16[4,128,640]{2,1,0:T(8,128)(2,1)S(1)} %gather_fusion), kind=kOutput, calls=%fused_computation.2 | convolution fusion | flops 591216640 | bytes 2719744 | tf_op jit(solution)/shard_map/kti,ktv->kiv/dot_general | solution.py:53
  (8 shorter events, 0.1 us)
Async XLA Ops:
  8.0 44.8 %copy-start = (bf16[128,3584]{1,0:T(8,128)(2,1)S(1)}, bf16[128,3584]{1,0:T(8,128)(2,1)}, u32[]{:S(2)}) copy-start(bf16[128,3584]{1,0:T(8,128)(2,1)} %param.5) | copy-start | bytes 2752516
  8.0 137.0 %reduce-scatter.4.cloned.1.call-start = ((), (), s32[]{:S(2)}) async-start(), calls=%async_computation.2 | async-start | bytes 2064384
  81.0 65.9 %all-gather.2.cloned.1.call-start = ((), (), s32[]{:S(2)}) async-start(), calls=%async_computation.1 | async-start | bytes 4587520 | tf_op jit(solution)/shard_map/all_gather | solution.py:49
  81.6 4.8 %collective-permute-start = (bf16[128,640]{1,0:T(8,128)(2,1)S(1)}, bf16[128,640]{1,0:T(8,128)(2,1)S(1)}, u32[]{:S(2)}, u32[]{:S(2)}) collective-permute-start(bf16[128,640]{1,0:T(8,128)(2,1)S(1)} %multiply_convert_fusion), channel_id=1, source_target_pairs={{0,8},{8,16},{16,24},{24,0},{1,9},{9,17},{17,25},{25,1},{2,10},{10... | collective-permute-start | bytes 491528 | tf_op jit(solution)/shard_map/ppermute | solution.py:21
  86.4 5.9 %collective-permute-start.1 = (bf16[128,640]{1,0:T(8,128)(2,1)S(1)}, bf16[128,640]{1,0:T(8,128)(2,1)S(1)}, u32[]{:S(2)}, u32[]{:S(2)}) collective-permute-start(bf16[128,640]{1,0:T(8,128)(2,1)S(1)} %collective-permute-done), channel_id=1, source_target_pairs={{0,8},{8,16},{16,24},{24,0},{1,9},{9,17},{17,25},{25,1},{2,10},{10... | collective-permute-start | bytes 491528 | tf_op jit(solution)/shard_map/ppermute | solution.py:21
  92.2 8.4 %collective-permute-start.2 = (bf16[128,640]{1,0:T(8,128)(2,1)S(1)}, bf16[128,640]{1,0:T(8,128)(2,1)S(1)}, u32[]{:S(2)}, u32[]{:S(2)}) collective-permute-start(bf16[128,640]{1,0:T(8,128)(2,1)S(1)} %collective-permute-done.1), channel_id=1, source_target_pairs={{0,8},{8,16},{16,24},{24,0},{1,9},{9,17},{17,25},{25,1},{2,10},{10... | collective-permute-start | bytes 491528 | tf_op jit(solution)/shard_map/ppermute | solution.py:21
Sparse Core Ops, SparseCore 0:
  81.1 63.8 reduce-scatter.3
Sparse Core Ops, SparseCore 1:
  83.0 31.0 all-gather.1
